TPU v7x, 32 devices: a whole 2x2x4 slice. The times are simulated.
32 devices in a mesh: dp: 8 (over y, x, core), seq: 4 (over z).
Axes of the slice: x: 2, y: 2, z: 4, core: 2. Of those that a mesh axis runs over, the one named last changes fastest.
Arguments:
- hidden: bfloat16 [8192, 1792], P(('dp', 'seq')), may hold values from -12.75 to 12.75
- depths: int32 [8192], P(('dp', 'seq')), may hold values from 1 to 3, as said below
- packed_slot_index: int32 [8192], P(('dp', 'seq')), may hold values from -1 to 511, as said below
- value_weight: bfloat16 [1792, 1024], P('dp'), may hold values from -0.125 to 0.125
- output_weight: bfloat16 [1024, 1792], P('dp'), may hold values from -0.1875 to 0.1875
- adapter_down_factor: bfloat16 [1792, 128], P('dp'), may hold values from -0.125 to 0.125
- adapter_up_factor: bfloat16 [1024, 128], P('dp'), may hold values from -0.5 to 0.5
- before_norm_gain: float32 [1792], replicated, may hold values from 0.1 to 1.9
- after_norm_gain: float32 [1792], replicated, may hold values from 0.1 to 1.9
- cotangent: bfloat16 [4096, 1792], P(('dp', 'seq')), may hold values from -6 to 6
Outputs:
- looped: bfloat16 [4096, 1792], P(('dp', 'seq'))
- grad_hidden: bfloat16 [8192, 1792], P(('dp', 'seq'))
- down_factor_gradient: float32 [1792, 128], P('dp', 'seq')
- up_factor_gradient: float32 [1024, 128], P('dp', 'seq')
Inputs may be any that keep to these rules, and one draw needn't show every extreme that they name: `depths`: of the 1024 tokens of one dp index exactly 512 have depth 2 or 3, and all 256 tokens of one seq index are among them. -1 exactly where depths is 1. Over the tokens of one dp index with depth 2 or 3 the slots are a permutation of 0 to 511; packed_slot_index // 128 is the seq index that holds the token's packed row. At most 64 tokens of one device have slots of one seq index, and exactly 64 do in every dp index.
All inputs are finite; a program needn't handle non-finite values.
Results may differ from a plain program's by a relative error of at most 0.01.
Values may be sent and summed in bfloat16 or wider, within the bound.
A program may use at most 64 MiB of HBM per device.

v0:
```python
import math
import jax
import jax.numpy as jnp
from jax import lax
from jax.sharding import PartitionSpec as P

epsilon = 1e-06


def contract_final_axis(left, right):
    return lax.dot_general(
        left, right, (((1,), (1,)), ((), ())), preferred_element_type=jnp.float32
    )


def contract_first(left, right):
    return lax.dot_general(
        left, right, (((0,), (0,)), ((), ())), preferred_element_type=jnp.float32
    )


def layer_forward(
    input_rows,
    cotangent_rows,
    value_weight,
    output_weight,
    adapter_down_factor,
    adapter_up_factor,
    before_norm_gain,
    after_norm_gain,
):
    x_float = input_rows.astype(jnp.float32)
    inv_pre = lax.rsqrt(jnp.mean(x_float * x_float, axis=-1, keepdims=True) + epsilon)
    whitened = x_float * inv_pre
    normalized_rows = (whitened * before_norm_gain).astype(jnp.bfloat16)
    rank_reduced = jnp.dot(
        normalized_rows, adapter_down_factor, preferred_element_type=jnp.float32
    ).astype(jnp.bfloat16)
    projected_rows = (
        jnp.dot(normalized_rows, value_weight, preferred_element_type=jnp.float32)
        + contract_final_axis(rank_reduced, adapter_up_factor)
    ).astype(jnp.bfloat16)
    mixed_out = jnp.dot(projected_rows, output_weight, preferred_element_type=jnp.float32)
    inv_post = lax.rsqrt(jnp.mean(mixed_out * mixed_out, axis=-1, keepdims=True) + epsilon)
    shaped = mixed_out * inv_post
    looped = (x_float + shaped * after_norm_gain).astype(jnp.bfloat16)
    cot_float = cotangent_rows.astype(jnp.float32)
    grad_shaped = cot_float * after_norm_gain
    grad_mixed = (
        inv_post * (grad_shaped - shaped * jnp.mean(grad_shaped * shaped, axis=-1, keepdims=True))
    ).astype(jnp.bfloat16)
    value_gradient = contract_final_axis(grad_mixed, output_weight).astype(jnp.bfloat16)
    low_rank_gradient = jnp.dot(
        value_gradient, adapter_up_factor, preferred_element_type=jnp.float32
    ).astype(jnp.bfloat16)
    normalized_gradient = contract_final_axis(value_gradient, value_weight) + contract_final_axis(
        low_rank_gradient, adapter_down_factor
    )
    grad_white = normalized_gradient * before_norm_gain
    gradient_rows = (
        cot_float
        + inv_pre
        * (grad_white - whitened * jnp.mean(grad_white * whitened, axis=-1, keepdims=True))
    ).astype(jnp.bfloat16)
    down_factor_gradient = contract_first(normalized_rows, low_rank_gradient)
    up_factor_gradient = contract_first(value_gradient, rank_reduced)
    return (looped, gradient_rows, down_factor_gradient, up_factor_gradient)


def body(
    hidden,
    depths,
    packed_slot_index,
    value_weight,
    output_weight,
    adapter_down_factor,
    adapter_up_factor,
    before_norm_gain,
    after_norm_gain,
    cotangent,
):
    seq_count = lax.axis_size("seq")
    own_index = lax.axis_index("seq")
    tok_count = hidden.shape[0]
    act_rows = cotangent.shape[0]
    value_full, out_full, down_full, up_full = (
        lax.all_gather(value_weight, "dp", axis=0, tiled=True),
        lax.all_gather(output_weight, "dp", axis=0, tiled=True),
        lax.all_gather(adapter_down_factor, "dp", axis=0, tiled=True),
        lax.all_gather(adapter_up_factor, "dp", axis=0, tiled=True),
    )
    depth_all, slot_all = (
        lax.all_gather(depths, "seq", axis=0, tiled=True),
        lax.all_gather(packed_slot_index, "seq", axis=0, tiled=True),
    )
    active_all = depth_all >= 2
    dest_all = jnp.where(active_all, slot_all // act_rows, -1)
    pos_all = jnp.where(active_all, slot_all % act_rows, 0)
    mine = active_all & (dest_all == own_index)
    active = depths >= 2
    zero_row = jnp.zeros((), jnp.bfloat16)
    rows_all = lax.all_gather(hidden, "seq", axis=0, tiled=True)
    source = (
        jnp.zeros((act_rows,), jnp.int32)
        .at[jnp.where(mine, pos_all, act_rows)]
        .set(jnp.arange(seq_count * tok_count, dtype=jnp.int32), mode="drop")
    )
    packed = jnp.take(rows_all, source, axis=0)
    looped, gradient_rows, down_factor_gradient, up_factor_gradient = layer_forward(
        packed,
        cotangent,
        value_full,
        out_full,
        down_full,
        up_full,
        before_norm_gain,
        after_norm_gain,
    )
    grads_all = lax.all_gather(gradient_rows, "seq", axis=0, tiled=True)
    picked = jnp.take(grads_all, jnp.maximum(packed_slot_index, 0), axis=0)
    grad_hidden = jnp.where(active[:, None], picked, zero_row)
    grad_scale = 1.0 / math.sqrt(seq_count * act_rows * lax.axis_size("dp"))
    down_term = down_factor_gradient * grad_scale
    up_term = up_factor_gradient * grad_scale
    down_mid, up_mid = (
        lax.psum_scatter(
            down_term.astype(jnp.bfloat16), "seq", scatter_dimension=1, tiled=True
        ).astype(jnp.float32),
        lax.psum_scatter(
            up_term.astype(jnp.bfloat16), "seq", scatter_dimension=1, tiled=True
        ).astype(jnp.float32),
    )
    down_sum, up_sum = (
        lax.psum_scatter(down_mid, "dp", scatter_dimension=0, tiled=True),
        lax.psum_scatter(up_mid, "dp", scatter_dimension=0, tiled=True),
    )
    return (looped, grad_hidden, down_sum, up_sum)


def solution(mesh):
    placed = (
        P(("dp", "seq"), None),
        P(("dp", "seq")),
        P(("dp", "seq")),
        P("dp", None),
        P("dp", None),
        P("dp", None),
        P("dp", None),
        P(),
        P(),
        P(("dp", "seq"), None),
    )
    return jax.shard_map(
        body,
        mesh=mesh,
        in_specs=placed,
        out_specs=(P(("dp", "seq"), None), P(("dp", "seq"), None), P("dp", "seq"), P("dp", "seq")),
        check_vma=False,
    )
```

profile of v0, /device:TPU:0, one launch (start us, length us, event | category | flops | bytes accessed | tf_op | source)
XLA Modules:
  0.0 329.3 jit_solution(13722843027043391828)
XLA Ops:
  9.4 12.8 %all-gather = s32[4,1,256]{2,1,0:T(1,128)S(1)} all-gather(s32[1,1,256]{2,1,0:T(1,128)} %bitcast.21), channel_id=1, replica_groups=mesh['dp'=8,'seq'=4] {'seq'}, dimensions={0}, use_global_device_ids=true | all-gather | bytes 5120 | tf_op jit(solution)/shard_map/all_gather | solution.py:93
  22.3 8.1 %all-gather.1 = s32[4,1,256]{2,1,0:T(1,128)S(1)} all-gather(s32[1,1,256]{2,1,0:T(1,128)} %bitcast.20), channel_id=1, replica_groups=mesh['dp'=8,'seq'=4] {'seq'}, dimensions={0}, use_global_device_ids=true | all-gather | bytes 5120 | tf_op jit(solution)/shard_map/all_gather | solution.py:94
  30.4 4.3 %scatter_custom_fusion = s32[128]{0:T(128)S(1)} fusion(s32[1024]{0:T(1024)S(1)} %compare_select_fusion, s32[1024]{0:T(1024)S(1)} %iota.3, s32[]{:T(128)} %constant.69.clone.1), kind=kCustom, calls=%fused_computation.69 | custom fusion | bytes 516 | tf_op jit(solution)/shard_map/scatter | solution.py:106
  34.8 9.5 %all_gather.29 = bf16[1024,128]{1,0:T(8,128)(2,1)S(1)} all-gather(bf16[128,128]{1,0:T(8,128)(2,1)} %param.16), channel_id=1, replica_groups=mesh['dp'=8,'seq'=4] {'dp'}, dimensions={0}, use_global_device_ids=true | all-gather | bytes 294912 | tf_op jit(solution)/shard_map/all_gather | solution.py:90
  44.3 9.5 %all_gather.28 = bf16[1792,128]{1,0:T(8,128)(2,1)S(1)} all-gather(bf16[224,128]{1,0:T(8,128)(2,1)} %param.15), channel_id=1, replica_groups=mesh['dp'=8,'seq'=4] {'dp'}, dimensions={0}, use_global_device_ids=true | all-gather | bytes 516096 | tf_op jit(solution)/shard_map/all_gather | solution.py:89
  53.8 30.7 %all-gather.7.cloned.1.call-done = bf16[1024,1792]{1,0:T(8,128)(2,1)} async-done(((bf16[256,1792]{1,0:T(8,128)(2,1)}), bf16[1024,1792]{1,0:T(8,128)(2,1)}) %all-gather.7.cloned.1.call-update) | async-done | bytes 3670032 | tf_op jit(solution)/shard_map/all_gather | solution.py:102
  84.5 3.8 %gather_fusion = bf16[128,1792]{1,0:T(8,128)(2,1)S(1)} fusion(bf16[1024,1792]{1,0:T(8,128)(2,1)} %all-gather.7.cloned.1.call-done, s32[1024]{0:T(1024)S(1)} %pad_clamp_fusion.1), kind=kCustom, calls=%fused_computation | custom fusion | bytes 918016 | tf_op jit(solution)/shard_map/jit(_take)/gather | solution.py:108
  89.0 30.5 %all-gather.9.cloned.1.call-done = bf16[1792,1024]{1,0:T(8,128)(2,1)} async-done(((bf16[224,1024]{1,0:T(8,128)(2,1)}), bf16[1792,1024]{1,0:T(8,128)(2,1)}) %all-gather.9.cloned.1.call-update) | async-done | bytes 3670032 | tf_op jit(solution)/shard_map/all_gather | solution.py:87
  119.5 2.7 fusion.37
  122.3 33.7 %all-gather.11.cloned.1.call-done = bf16[1024,1792]{1,0:T(8,128)(2,1)} async-done(((bf16[128,1792]{1,0:T(8,128)(2,1)}), bf16[1024,1792]{1,0:T(8,128)(2,1)}) %all-gather.11.cloned.1.call-update) | async-done | bytes 3670032 | tf_op jit(solution)/shard_map/all_gather | solution.py:88
  156.0 2.9 multiply_reduce_fusion
  160.0 3.4 %convolution_convert_fusion = bf16[128,1024]{1,0:T(8,128)(2,1)S(1)} fusion(bf16[1024,1792]{1,0:T(8,128)(2,1)} %all-gather.11.cloned.1.call-done, bf16[128,1792]{1,0:T(8,128)(2,1)S(1)} %copy-done, f32[128,1792]{1,0:T(8,128)S(1)} %get-tuple-element.7, f32[128]{0:T(128)S(1)} %broadcast_multiply_fusion.1, f32[1792]{0:T(1024)S(1)} %copy-done.1, ...), kind=kOutput, calls=%fused_computation.15 | convolution fusion | flops 471498752 | bytes 5316608 | tf_op jit(solution)/shard_map/dot_general | solution.py:11
  163.6 1.2 fusion.1
  165.9 3.4 %fusion.39 = f32[128,1792]{1,0:T(8,128)S(1)} fusion(bf16[128,1024]{1,0:T(8,128)(2,1)S(1)} %convolution_convert_fusion, bf16[1792,1024]{1,0:T(8,128)(2,1)} %all-gather.9.cloned.1.call-done), kind=kOutput, calls=%fused_computation.72 | convolution fusion | flops 469762048 | bytes 4849664 | tf_op jit(solution)/shard_map/dot_general | solution.py:11
  169.8 16.2 %reduce-scatter.7.cloned.1.call-done = bf16[1792,32]{0,1:T(8,128)(2,1)} async-done(((bf16[1792,128]{0,1:T(8,128)(2,1)}), bf16[1792,32]{0,1:T(8,128)(2,1)}) %reduce-scatter.7.cloned.1.call-update) | async-done | bytes 114704 | tf_op jit(solution)/shard_map/reduce_scatter | solution.py:126
  186.0 2.0 copy.14
  188.1 1.3 fusion.13
  189.6 16.7 %reduce-scatter.9.cloned.1.call-done = bf16[1024,32]{0,1:T(8,128)(2,1)} async-done(((bf16[1024,128]{0,1:T(8,128)(2,1)}), bf16[1024,32]{0,1:T(8,128)(2,1)}) %reduce-scatter.9.cloned.1.call-update) | async-done | bytes 65552 | tf_op jit(solution)/shard_map/reduce_scatter | solution.py:129
  206.3 1.5 convert_element_type.55
  207.8 35.8 %reduce-scatter.13.cloned.1.call-done = f32[224,32]{1,0:T(8,128)} async-done(((f32[1792,32]{1,0:T(8,128)}), f32[224,32]{1,0:T(8,128)}) %reduce-scatter.13.cloned.1.call-update) | async-done | bytes 28688
  243.6 1.6 copy.15
  245.2 41.4 %all-gather.13.cloned.1.call-done = bf16[512,1792]{1,0:T(8,128)(2,1)} async-done(((bf16[128,1792]{1,0:T(8,128)(2,1)}), bf16[512,1792]{1,0:T(8,128)(2,1)}) %all-gather.13.cloned.1.call-update) | async-done | bytes 1835024 | tf_op jit(solution)/shard_map/all_gather | solution.py:119
  286.6 3.9 %gather_fusion.1 = bf16[256,1792]{1,0:T(8,128)(2,1)S(1)} fusion(bf16[512,1792]{1,0:T(8,128)(2,1)} %all-gather.13.cloned.1.call-done, s32[1024]{0:T(1024)S(1)} %pad_clamp_fusion), kind=kCustom, calls=%fused_computation.1 | custom fusion | bytes 1836032 | tf_op jit(solution)/shard_map/jit(_take)/gather | solution.py:120
  291.6 30.8 %reduce-scatter.11.cloned.1.call-done = f32[128,32]{0,1:T(8,128)} async-done(((f32[1024,32]{0,1:T(8,128)}), f32[128,32]{0,1:T(8,128)}) %reduce-scatter.11.cloned.1.call-update) | async-done | bytes 16400 | tf_op jit(solution)/shard_map/reduce_scatter | solution.py:135
  (48 shorter events, 7.1 us)
Async XLA Ops:
  7.2 81.5 %copy-start.2 = (f32[1792]{0:T(1024)S(1)}, f32[1792]{0:T(1024)}, u32[]{:S(2)}) copy-start(f32[1792]{0:T(1024)} %param.17) | copy-start | bytes 21508
  7.2 77.3 %all-gather.7.cloned.1.call-start = ((), (), s32[]{:S(2)}) async-start(), calls=%async_computation.4 | async-start | bytes 4587520 | tf_op jit(solution)/shard_map/all_gather | solution.py:102
  7.9 111.6 %all-gather.9.cloned.1.call-start = ((), (), s32[]{:S(2)}) async-start(), calls=%async_computation.5 | async-start | bytes 4128768 | tf_op jit(solution)/shard_map/all_gather | solution.py:87
  8.7 147.3 %all-gather.11.cloned.1.call-start = ((), (), s32[]{:S(2)}) async-start(), calls=%async_computation.6 | async-start | bytes 4128768 | tf_op jit(solution)/shard_map/all_gather | solution.py:88
  9.4 176.6 %reduce-scatter.7.cloned.1.call-start = ((), (), s32[]{:S(2)}) async-start(), calls=%async_computation.8 | async-start | bytes 573440 | tf_op jit(solution)/shard_map/reduce_scatter | solution.py:126
  122.3 36.7 %copy-start = (bf16[128,1792]{1,0:T(8,128)(2,1)S(1)}, bf16[128,1792]{1,0:T(8,128)(2,1)}, u32[]{:S(2)}) copy-start(bf16[128,1792]{1,0:T(8,128)(2,1)} %param.19) | copy-start | bytes 1376260
  122.3 36.6 %copy-start.1 = (f32[1792]{0:T(1024)S(1)}, f32[1792]{0:T(1024)}, u32[]{:S(2)}) copy-start(f32[1792]{0:T(1024)} %param.18) | copy-start | bytes 21508
  164.8 41.5 %reduce-scatter.9.cloned.1.call-start = ((), (), s32[]{:S(2)}) async-start(), calls=%async_computation.9 | async-start | bytes 327680 | tf_op jit(solution)/shard_map/reduce_scatter | solution.py:129
  165.8 77.8 %reduce-scatter.13.cloned.1.call-start = ((), (), s32[]{:S(2)}) async-start(), calls=%async_computation.11 | async-start | bytes 1032192
  169.3 20.2 %copy-start.3 = (s32[256]{0:T(256)S(1)}, s32[256]{0:T(256)}, u32[]{:S(2)}) copy-start(s32[256]{0:T(256)} %param.12) | copy-start | bytes 3076
  169.3 20.3 %copy-start.4 = (s32[256]{0:T(256)S(1)}, s32[256]{0:T(256)}, u32[]{:S(2)}) copy-start(s32[256]{0:T(256)} %param.11) | copy-start | bytes 3076
  188.0 98.6 %all-gather.13.cloned.1.call-start = ((), (), s32[]{:S(2)}) async-start(), calls=%async_computation.7 | async-start | bytes 2293760 | tf_op jit(solution)/shard_map/all_gather | solution.py:119
  189.4 133.0 %reduce-scatter.11.cloned.1.call-start = ((), (), s32[]{:S(2)}) async-start(), calls=%async_computation.10 | async-start | bytes 147456 | tf_op jit(solution)/shard_map/reduce_scatter | solution.py:135
Sparse Core Ops, SparseCore 0:
  9.6 74.8 all-gather.6
  86.4 33.0 all-gather.8
  121.4 34.5 all-gather.10
  164.9 20.9 reduce-scatter.6
  188.2 18.0 reduce-scatter.8
  209.9 33.6 reduce-scatter.12
  245.2 41.3 all-gather.12
  290.2 32.2 reduce-scatter.10
where the time goes:
time: 330 us; the launch traced here: 329 us
  waiting for transfers between devices  238 us (72%)
  blocking collectives  39.9 us (12%)
  local copies, waits for them, and re-layouts  15.7 us (5%)
  matrix products  15.5 us (5%)
  between operations  14.3 us (4%)
  other arithmetic  5.43 us (2%)
    all_gather x1, waiting for transfers between devices, body(): grads_all = lax.all_gather(gradient_rows, 'seq', axis=0, tiled=True)  41.4 us
    unnamed x9, waiting for transfers between devices  38 us
    all_gather x1, waiting for transfers between devices, body(): lax.all_gather(output_weight, 'dp', axis=0, tiled=True)  33.7 us
    reduce_scatter x1, waiting for transfers between devices, body(): lax.psum_scatter(up_mid, 'dp', scatter_dimension=0, tiled=True)  30.8 us
    all_gather x1, waiting for transfers between devices, body(): rows_all = lax.all_gather(hidden, 'seq', axis=0, tiled=True)  30.7 us
    all_gather x1, waiting for transfers between devices, body(): lax.all_gather(value_weight, 'dp', axis=0, tiled=True)  30.5 us
    reduce_scatter x1, waiting for transfers between devices, body(): lax.psum_scatter(up_term.astype(jnp.bfloat16), 'seq', scatter_dimension=1...  16.7 us
    reduce_scatter x1, waiting for transfers between devices, body(): lax.psum_scatter(down_term.astype(jnp.bfloat16), 'seq', scatter_dimension...  16.2 us
  transfers between devices with their start and end apart: 8, of which 8 were waited for; matrix products, arithmetic and copies ran while one was open for 8% of the time, Pallas kernels for 0%

commit v1 on v0

--- a/solution.py
+++ b/solution.py
@@ -5,6 +5,15 @@
 from jax.sharding import PartitionSpec as P
 
 epsilon = 1e-06
+post_patch_here = lambda local_array: jnp.concatenate(
+    lax.all_to_all(
+        jnp.stack([local_array for _ in range(lax.psum(1, axis_name="seq"))]),
+        axis_name="seq",
+        split_axis=0,
+        concat_axis=0,
+    ),
+    axis=0,
+)
 
 
 def contract_final_axis(left, right):
@@ -90,7 +99,7 @@
         lax.all_gather(adapter_up_factor, "dp", axis=0, tiled=True),
     )
     depth_all, slot_all = (
-        lax.all_gather(depths, "seq", axis=0, tiled=True),
+        post_patch_here(depths),
         lax.all_gather(packed_slot_index, "seq", axis=0, tiled=True),
     )
     active_all = depth_all >= 2

time: 330 us -> 330 us (level)
  blocking collectives: 39.9 us -> 30.8 us
  starting transfers between devices: 0.32 us -> 6.6 us
    all_gather x1 -> x0, blocking collectives: 12.8 us -> none  [body(): lax.all_gather(depths, 'seq', axis=0, tiled=True)]
    all_to_all x0 -> x1, starting transfers between devices: none -> 6.32 us  [lax.all_to_all(jnp.stack([local_array for _ in range(lax.psum(1, axis_nam...]
    all_gather x1, blocking collectives: 8.08 us -> 11.8 us  [body(): lax.all_gather(packed_slot_index, 'seq', axis=0, tiled=True)]
  transfers between devices with their start and end apart: 8 -> 9, of which waited for: 8 -> 8; matrix products, arithmetic and copies ran while one was open for 8% -> 9% of each run, Pallas kernels for 0% -> 0%
where the time goes in v1:
time: 330 us; the launch traced here: 329 us
  waiting for transfers between devices  240 us (73%)
  blocking collectives  30.8 us (9%)
  local copies, waits for them, and re-layouts  17 us (5%)
  matrix products  15.5 us (5%)
  between operations  14.3 us (4%)
  starting transfers between devices  6.6 us (2%)
  other arithmetic  5.44 us (2%)
    all_gather x1, waiting for transfers between devices, body(): grads_all = lax.all_gather(gradient_rows, 'seq', axis=0, tiled=True)  41.4 us
    unnamed x9, waiting for transfers between devices  38 us
    all_gather x1, waiting for transfers between devices, body(): lax.all_gather(output_weight, 'dp', axis=0, tiled=True)  33.7 us
    all_gather x1, waiting for transfers between devices, body(): rows_all = lax.all_gather(hidden, 'seq', axis=0, tiled=True)  32.3 us
    reduce_scatter x1, waiting for transfers between devices, body(): lax.psum_scatter(up_mid, 'dp', scatter_dimension=0, tiled=True)  30.8 us
    all_gather x1, waiting for transfers between devices, body(): lax.all_gather(value_weight, 'dp', axis=0, tiled=True)  30.6 us
    reduce_scatter x1, waiting for transfers between devices, body(): lax.psum_scatter(up_term.astype(jnp.bfloat16), 'seq', scatter_dimension=1...  16.7 us
    reduce_scatter x1, waiting for transfers between devices, body(): lax.psum_scatter(down_term.astype(jnp.bfloat16), 'seq', scatter_dimension...  16.2 us
  transfers between devices with their start and end apart: 9, of which 8 were waited for; matrix products, arithmetic and copies ran while one was open for 9% of the time, Pallas kernels for 0%

profile of v1, /device:TPU:0, one launch (start us, length us, event | category | flops | bytes accessed | tf_op | source)
XLA Modules:
  0.0 329.4 jit_solution(14723840790087526818)
XLA Ops:
  9.4 1.3 stack.2
  10.7 6.3 %all-to-all-start = ((s32[4,1,256]{2,1,0:T(1,128)}), s32[4,1,256]{2,1,0:T(1,128)S(1)}, u32[]{:S(2)}, u32[]{:S(2)}) async-start(s32[4,1,256]{2,1,0:T(1,128)} %stack.2), calls=%async_computation | async-start | bytes 8192 | tf_op jit(solution)/shard_map/all_to_all | solution.py:9
  17.0 10.0 %all_gather.24 = bf16[1792,128]{1,0:T(8,128)(2,1)S(1)} all-gather(bf16[224,128]{1,0:T(8,128)(2,1)} %param.15), channel_id=1, replica_groups=mesh['dp'=8,'seq'=4] {'dp'}, dimensions={0}, use_global_device_ids=true | all-gather | bytes 516096 | tf_op jit(solution)/shard_map/all_gather | solution.py:98
  27.0 9.0 %all_gather.25 = bf16[1024,128]{1,0:T(8,128)(2,1)S(1)} all-gather(bf16[128,128]{1,0:T(8,128)(2,1)} %param.16), channel_id=1, replica_groups=mesh['dp'=8,'seq'=4] {'dp'}, dimensions={0}, use_global_device_ids=true | all-gather | bytes 294912 | tf_op jit(solution)/shard_map/all_gather | solution.py:99
  36.0 11.8 %all-gather = s32[4,1,256]{2,1,0:T(1,128)S(1)} all-gather(s32[1,1,256]{2,1,0:T(1,128)} %bitcast.19), channel_id=1, replica_groups=mesh['dp'=8,'seq'=4] {'seq'}, dimensions={0}, use_global_device_ids=true | all-gather | bytes 5120 | tf_op jit(solution)/shard_map/all_gather | solution.py:103
  47.8 4.3 %scatter_custom_fusion = s32[128]{0:T(128)S(1)} fusion(s32[1024]{0:T(1024)S(1)} %compare_select_fusion, s32[1024]{0:T(1024)S(1)} %iota.3, s32[]{:T(128)} %constant.69.clone.1), kind=kCustom, calls=%fused_computation.69 | custom fusion | bytes 516 | tf_op jit(solution)/shard_map/scatter | solution.py:115
  52.2 32.3 %all-gather.6.cloned.1.call-done = bf16[1024,1792]{1,0:T(8,128)(2,1)} async-done(((bf16[256,1792]{1,0:T(8,128)(2,1)}), bf16[1024,1792]{1,0:T(8,128)(2,1)}) %all-gather.6.cloned.1.call-update) | async-done | bytes 3670032 | tf_op jit(solution)/shard_map/all_gather | solution.py:111
  84.5 3.8 %gather_fusion = bf16[128,1792]{1,0:T(8,128)(2,1)S(1)} fusion(bf16[1024,1792]{1,0:T(8,128)(2,1)} %all-gather.6.cloned.1.call-done, s32[1024]{0:T(1024)S(1)} %pad_clamp_fusion.1), kind=kCustom, calls=%fused_computation | custom fusion | bytes 918016 | tf_op jit(solution)/shard_map/jit(_take)/gather | solution.py:117
  89.0 30.6 %all-gather.8.cloned.1.call-done = bf16[1792,1024]{1,0:T(8,128)(2,1)} async-done(((bf16[224,1024]{1,0:T(8,128)(2,1)}), bf16[1792,1024]{1,0:T(8,128)(2,1)}) %all-gather.8.cloned.1.call-update) | async-done | bytes 3670032 | tf_op jit(solution)/shard_map/all_gather | solution.py:96
  119.5 2.7 fusion.37
  122.3 33.7 %all-gather.10.cloned.1.call-done = bf16[1024,1792]{1,0:T(8,128)(2,1)} async-done(((bf16[128,1792]{1,0:T(8,128)(2,1)}), bf16[1024,1792]{1,0:T(8,128)(2,1)}) %all-gather.10.cloned.1.call-update) | async-done | bytes 3670032 | tf_op jit(solution)/shard_map/all_gather | solution.py:97
  156.0 2.9 multiply_reduce_fusion
  160.0 3.4 %convolution_convert_fusion = bf16[128,1024]{1,0:T(8,128)(2,1)S(1)} fusion(bf16[1024,1792]{1,0:T(8,128)(2,1)} %all-gather.10.cloned.1.call-done, bf16[128,1792]{1,0:T(8,128)(2,1)S(1)} %copy-done, f32[128,1792]{1,0:T(8,128)S(1)} %get-tuple-element.7, f32[128]{0:T(128)S(1)} %broadcast_multiply_fusion.1, f32[1792]{0:T(1024)S(1)} %copy-done.1, ...), kind=kOutput, calls=%fused_computation.15 | convolution fusion | flops 471498752 | bytes 5316608 | tf_op jit(solution)/shard_map/dot_general | solution.py:20
  165.9 3.4 %fusion.39 = f32[128,1792]{1,0:T(8,128)S(1)} fusion(bf16[128,1024]{1,0:T(8,128)(2,1)S(1)} %convolution_convert_fusion, bf16[1792,1024]{1,0:T(8,128)(2,1)} %all-gather.8.cloned.1.call-done), kind=kOutput, calls=%fused_computation.72 | convolution fusion | flops 469762048 | bytes 4849664 | tf_op jit(solution)/shard_map/dot_general | solution.py:20
  169.8 16.2 %reduce-scatter.7.cloned.1.call-done = bf16[1792,32]{0,1:T(8,128)(2,1)} async-done(((bf16[1792,128]{0,1:T(8,128)(2,1)}), bf16[1792,32]{0,1:T(8,128)(2,1)}) %reduce-scatter.7.cloned.1.call-update) | async-done | bytes 114704 | tf_op jit(solution)/shard_map/reduce_scatter | solution.py:135
  186.0 2.0 copy.14
  188.1 1.4 fusion.13
  189.6 16.7 %reduce-scatter.9.cloned.1.call-done = bf16[1024,32]{0,1:T(8,128)(2,1)} async-done(((bf16[1024,128]{0,1:T(8,128)(2,1)}), bf16[1024,32]{0,1:T(8,128)(2,1)}) %reduce-scatter.9.cloned.1.call-update) | async-done | bytes 65552 | tf_op jit(solution)/shard_map/reduce_scatter | solution.py:138
  206.3 1.5 convert_element_type.55
  207.8 35.9 %reduce-scatter.13.cloned.1.call-done = f32[224,32]{1,0:T(8,128)} async-done(((f32[1792,32]{1,0:T(8,128)}), f32[224,32]{1,0:T(8,128)}) %reduce-scatter.13.cloned.1.call-update) | async-done | bytes 28688
  243.7 1.6 copy.15
  245.3 41.4 %all-gather.12.cloned.1.call-done = bf16[512,1792]{1,0:T(8,128)(2,1)} async-done(((bf16[128,1792]{1,0:T(8,128)(2,1)}), bf16[512,1792]{1,0:T(8,128)(2,1)}) %all-gather.12.cloned.1.call-update) | async-done | bytes 1835024 | tf_op jit(solution)/shard_map/all_gather | solution.py:128
  286.7 3.9 %gather_fusion.1 = bf16[256,1792]{1,0:T(8,128)(2,1)S(1)} fusion(bf16[512,1792]{1,0:T(8,128)(2,1)} %all-gather.12.cloned.1.call-done, s32[1024]{0:T(1024)S(1)} %pad_clamp_fusion), kind=kCustom, calls=%fused_computation.1 | custom fusion | bytes 1836032 | tf_op jit(solution)/shard_map/jit(_take)/gather | solution.py:129
  291.7 30.8 %reduce-scatter.11.cloned.1.call-done = f32[128,32]{0,1:T(8,128)} async-done(((f32[1024,32]{0,1:T(8,128)}), f32[128,32]{0,1:T(8,128)}) %reduce-scatter.11.cloned.1.call-update) | async-done | bytes 16400 | tf_op jit(solution)/shard_map/reduce_scatter | solution.py:144
  (50 shorter events, 8.2 us)
Async XLA Ops:
  7.2 81.4 %copy-start.2 = (f32[1792]{0:T(1024)S(1)}, f32[1792]{0:T(1024)}, u32[]{:S(2)}) copy-start(f32[1792]{0:T(1024)} %param.17) | copy-start | bytes 21508
  7.2 77.3 %all-gather.6.cloned.1.call-start = ((), (), s32[]{:S(2)}) async-start(), calls=%async_computation.5 | async-start | bytes 4587520 | tf_op jit(solution)/shard_map/all_gather | solution.py:111
  7.9 111.6 %all-gather.8.cloned.1.call-start = ((), (), s32[]{:S(2)}) async-start(), calls=%async_computation.6 | async-start | bytes 4128768 | tf_op jit(solution)/shard_map/all_gather | solution.py:96
  8.7 147.3 %all-gather.10.cloned.1.call-start = ((), (), s32[]{:S(2)}) async-start(), calls=%async_computation.7 | async-start | bytes 4128768 | tf_op jit(solution)/shard_map/all_gather | solution.py:97
  10.7 37.1 %all-to-all-start = ((s32[4,1,256]{2,1,0:T(1,128)}), s32[4,1,256]{2,1,0:T(1,128)S(1)}, u32[]{:S(2)}, u32[]{:S(2)}) async-start(s32[4,1,256]{2,1,0:T(1,128)} %stack.2), calls=%async_computation | async-start | bytes 8192 | tf_op jit(solution)/shard_map/all_to_all | solution.py:9
  17.0 169.0 %reduce-scatter.7.cloned.1.call-start = ((), (), s32[]{:S(2)}) async-start(), calls=%async_computation.9 | async-start | bytes 573440 | tf_op jit(solution)/shard_map/reduce_scatter | solution.py:135
  122.3 36.6 %copy-start = (bf16[128,1792]{1,0:T(8,128)(2,1)S(1)}, bf16[128,1792]{1,0:T(8,128)(2,1)}, u32[]{:S(2)}) copy-start(bf16[128,1792]{1,0:T(8,128)(2,1)} %param.19) | copy-start | bytes 1376260
  122.3 36.6 %copy-start.1 = (f32[1792]{0:T(1024)S(1)}, f32[1792]{0:T(1024)}, u32[]{:S(2)}) copy-start(f32[1792]{0:T(1024)} %param.18) | copy-start | bytes 21508
  164.8 41.5 %reduce-scatter.9.cloned.1.call-start = ((), (), s32[]{:S(2)}) async-start(), calls=%async_computation.10 | async-start | bytes 327680 | tf_op jit(solution)/shard_map/reduce_scatter | solution.py:138
  165.9 77.8 %reduce-scatter.13.cloned.1.call-start = ((), (), s32[]{:S(2)}) async-start(), calls=%async_computation.12 | async-start | bytes 1032192
  169.3 20.3 %copy-start.3 = (s32[256]{0:T(256)S(1)}, s32[256]{0:T(256)}, u32[]{:S(2)}) copy-start(s32[256]{0:T(256)} %param.12) | copy-start | bytes 3076
  169.3 20.3 %copy-start.4 = (s32[256]{0:T(256)S(1)}, s32[256]{0:T(256)}, u32[]{:S(2)}) copy-start(s32[256]{0:T(256)} %param.11) | copy-start | bytes 3076
  188.1 98.6 %all-gather.12.cloned.1.call-start = ((), (), s32[]{:S(2)}) async-start(), calls=%async_computation.8 | async-start | bytes 2293760 | tf_op jit(solution)/shard_map/all_gather | solution.py:128
  189.5 133.0 %reduce-scatter.11.cloned.1.call-start = ((), (), s32[]{:S(2)}) async-start(), calls=%async_computation.11 | async-start | bytes 147456 | tf_op jit(solution)/shard_map/reduce_scatter | solution.py:144
Sparse Core Ops, SparseCore 0:
  9.6 74.8 all-gather.5
  86.3 33.1 all-gather.7
  121.4 34.5 all-gather.9
  164.9 21.0 reduce-scatter.6
  188.2 18.0 reduce-scatter.8
  209.9 33.7 reduce-scatter.12
  245.3 41.3 all-gather.11
  290.2 32.2 reduce-scatter.10
